TPU v7x, 128 devices: a whole 4x4x4 slice. The times are simulated.
128 devices in a mesh: wide: 8 (over y, core), narrow: 16 (over z, x).
Axes of the slice: x: 4, y: 4, z: 4, core: 2. Of those that a mesh axis runs over, the one named last changes fastest.
Arguments:
- queries: bfloat16 [32768, 128], P(('wide', 'narrow')), may hold values from -6 to 6
- index_rows: bfloat16 [1048576, 128], P(('wide', 'narrow')), may hold values from -6 to 6
- lse_shift: float32 [32768], P('wide'), may hold values from 0 to 2.5
- loss_weight: float32 [32768], P('wide'), may hold values from 4 to 32
- positives: int32 [32768], P('wide'), may hold values from 0 to 131071
- tile_negs: int32 [256, 512], P('wide'), may hold values from 0 to 1023
- fetch_owner: int32 [8192, 1], P(('wide', 'narrow')), may hold values from 0 to 127; in each aligned block of 64 rows (0 to 63, 64 to 127, ...) at most 2 rows name the same one
- fetch_local: int32 [8192], P(('wide', 'narrow')), may hold values from 0 to 63
Outputs:
- query_grad: float32 [32768, 128], P(('wide', 'narrow'))
- index_grad: float32 [1048576, 128], P(('wide', 'narrow'))
Inputs may be any that keep to these rules, and one draw needn't show every extreme that they name: `fetch_owner`: among the 64 fetches of one device no owner is named more than 2 times, a bound that some block reaches.
All inputs are finite; a program needn't handle non-finite values.
Results may differ from a plain program's by a relative error of at most 0.0043.
Values may be sent and summed in bfloat16 or wider, within the bound.
No kernel may reach another device: no remote copies, remote signals or barrier semaphores. Data moves between devices by JAX's collectives and lax.ppermute only.
A program may use at most 128 MiB of HBM per device.

v0:
```python
import math
import jax
import jax.numpy as jnp
from jax import lax
from jax.sharding import PartitionSpec as P

BLOCK = 128
QTILE = 128
CAP = 2


def slot_places(owners):
    fetch_count = owners.shape[0]
    position = jnp.arange(fetch_count, dtype=jnp.int32)
    same_owner = (owners[:, None] == owners[None, :]) & (position[None, :] < position[:, None])
    before = jnp.sum(same_owner.astype(jnp.int32), axis=1)
    return owners * CAP + before


def shards(
    queries, index_rows, lse_shift, loss_weight, positives, tile_negs, fetch_owner, fetch_local
):
    wide_count = lax.axis_size("wide")
    narrow_count = lax.axis_size("narrow")
    slots_all = wide_count * narrow_count * CAP
    feat_width = queries.shape[1]
    blocks_here = index_rows.shape[0] // BLOCK
    owners = fetch_owner[:, 0]
    fetch_count = owners.shape[0]
    places = slot_places(owners)
    grouped = lax.all_gather(queries, "narrow", axis=0, tiled=True)
    requests = jnp.full((slots_all,), -1, jnp.int32).at[places].set(fetch_local)
    asked_ids = lax.all_to_all(
        requests, ("wide", "narrow"), split_axis=0, concat_axis=0, tiled=True
    )
    stored = index_rows.reshape(blocks_here, BLOCK, feat_width)
    served = jnp.take(stored, jnp.maximum(asked_ids, 0), axis=0)
    arrived = lax.all_to_all(served, ("wide", "narrow"), split_axis=0, concat_axis=0, tiled=True)
    fetched = jnp.take(arrived, places, axis=0).reshape(fetch_count * BLOCK, feat_width)
    score_scale = 2.0 / math.sqrt(feat_width)
    narrow_pos = lax.axis_index("narrow")
    query_total = grouped.shape[0]
    block_size = min(512, query_total)
    block_count = query_total // block_size
    column_count = fetch_count * BLOCK
    lse_full = lse_shift + math.log(fetch_count * narrow_count * BLOCK)
    slot_ids = narrow_pos * fetch_count + jnp.arange(fetch_count, dtype=jnp.int32)
    tile_hit = jnp.any(tile_negs[:, :, None] == slot_ids[None, None, :], axis=1)
    query_hit = jnp.repeat(tile_hit, QTILE, axis=0)
    pos_hit = (positives // BLOCK)[:, None] == slot_ids[None, :]
    query_weight = jnp.logical_or(query_hit, pos_hit).astype(jnp.float32)
    column_ids = narrow_pos * column_count + jnp.arange(column_count, dtype=jnp.int32)

    def one_block(turn_idx, totals):
        block_grad, query_grad = totals
        row_start = turn_idx * block_size
        query_block = lax.dynamic_slice_in_dim(grouped, row_start, block_size, 0)
        row_weight = lax.dynamic_slice_in_dim(query_weight, row_start, block_size, 0)
        lse_rows = lax.dynamic_slice_in_dim(lse_full, row_start, block_size, 0)
        loss_rows = lax.dynamic_slice_in_dim(loss_weight, row_start, block_size, 0)
        pos_rows = lax.dynamic_slice_in_dim(positives, row_start, block_size, 0)
        scores = (
            lax.dot_general(
                query_block, fetched, (((1,), (1,)), ((), ())), preferred_element_type=jnp.float32
            )
            * score_scale
        )
        softmax_terms = jnp.exp(scores - lse_rows[:, None])
        weighted = (
            softmax_terms.reshape(block_size, fetch_count, BLOCK) * row_weight[:, :, None]
        ).reshape(block_size, column_count)
        target = (pos_rows[:, None] == column_ids[None, :]).astype(jnp.float32)
        logit_grad = (loss_rows[:, None] * (weighted - target)).astype(jnp.bfloat16)
        query_part = jnp.dot(logit_grad, fetched, preferred_element_type=jnp.float32) * score_scale
        query_grad = lax.dynamic_update_slice_in_dim(query_grad, query_part, row_start, 0)
        block_grad = block_grad + lax.dot_general(
            logit_grad, query_block, (((0,), (0,)), ((), ())), preferred_element_type=jnp.float32
        )
        return (block_grad, query_grad)

    zeros_init = (
        jnp.zeros((column_count, feat_width), jnp.float32),
        jnp.zeros((query_total, feat_width), jnp.float32),
    )
    block_grad, query_grad = lax.fori_loop(0, block_count, one_block, zeros_init)
    block_send = (
        (block_grad * score_scale).astype(jnp.bfloat16).reshape(fetch_count, BLOCK, feat_width)
    )
    outgoing = jnp.zeros((slots_all, BLOCK, feat_width), jnp.bfloat16).at[places].set(block_send)
    returned = lax.all_to_all(outgoing, ("wide", "narrow"), split_axis=0, concat_axis=0, tiled=True)
    onehot = (asked_ids[None, :] == jnp.arange(blocks_here, dtype=jnp.int32)[:, None]).astype(
        jnp.bfloat16
    )
    index_grad = jnp.dot(
        onehot, returned.reshape(slots_all, BLOCK * feat_width), preferred_element_type=jnp.float32
    )
    index_grad = index_grad.reshape(blocks_here * BLOCK, feat_width)
    own_rows = queries.shape[0]
    summed = lax.psum(query_grad, "narrow")
    query_out = lax.dynamic_slice_in_dim(summed, narrow_pos * own_rows, own_rows, 0)
    return (query_out, index_grad)


def solution(mesh):
    in_specs = (
        P(("wide", "narrow"), None),
        P(("wide", "narrow"), None),
        P("wide"),
        P("wide"),
        P("wide"),
        P("wide", None),
        P(("wide", "narrow"), None),
        P(("wide", "narrow")),
    )
    out_specs = (P(("wide", "narrow"), None), P(("wide", "narrow"), None))
    return jax.shard_map(shards, mesh=mesh, in_specs=in_specs, out_specs=out_specs, check_vma=False)
```

profile of v0, /device:TPU:0, one launch (start us, length us, event | category | flops | bytes accessed | tf_op | source)
XLA Modules:
  0.0 723.2 jit_solution(15473368528226750024)
XLA Ops:
  9.9 20.5 %all_to_all.22 = s32[128,2,1]{1,2,0:T(1,128)S(1)} all-to-all(s32[128,2,1]{1,2,0:T(1,128)S(1)} %bitcast.53), channel_id=1, replica_groups=mesh['wide'=8,'narrow'=16] {'wide','narrow'}, dimensions={0} | all-to-all | bytes 2048 | tf_op jit(solution)/shard_map/all_to_all | solution.py:33
  32.2 8.3 %gather_fusion = bf16[256,128,128]{2,1,0:T(8,128)(2,1)} fusion(bf16[64,128,128]{2,1,0:T(8,128)(2,1)S(1)} %bitcast.50, s32[1024]{0:T(1024)S(1)} %pad_clamp_fusion.1), kind=kCustom, calls=%fused_computation | custom fusion | bytes 16778240 | tf_op jit(solution)/shard_map/jit(_take)/gather | solution.py:37
  40.6 7.4 %broadcast_select_fusion = bf16[256,128,128]{2,1,0:T(8,128)(2,1)} fusion(bf16[256,128,128]{2,1,0:T(8,128)(2,1)} %gather_fusion, pred[256]{0:T(512)(128)(4,1)S(1)} %maximum_compare_fusion), kind=kLoop, calls=%fused_computation.21 | loop fusion | flops 4194304 | bytes 16777472 | tf_op jit(solution)/shard_map/jit(_take)/select_n | solution.py:37
  57.5 95.4 %all-to-all-done.1 = bf16[256,128,128]{2,1,0:T(8,128)(2,1)} async-done(((bf16[256,128,128]{2,1,0:T(8,128)(2,1)}), bf16[256,128,128]{2,1,0:T(8,128)(2,1)}, u32[]{:S(2)}, u32[]{:S(2)}) %all-to-all-start.1) | async-done | bytes 8388640 | tf_op jit(solution)/shard_map/all_to_all | solution.py:38
  162.3 8.3 %all-gather.2.cloned.1.call-done = bf16[4096,128]{1,0:T(8,128)(2,1)} async-done(((bf16[256,128]{1,0:T(8,128)(2,1)}), bf16[4096,128]{1,0:T(8,128)(2,1)}) %all-gather.2.cloned.1.call-update) | async-done | bytes 1048592 | tf_op jit(solution)/shard_map/all_gather | solution.py:31
  172.0 325.2 %while.16 = (s32[]{:T(128)}, f32[8192,128]{1,0:T(8,128)}, f32[4096,128]{1,0:T(8,128)}, f32[4096]{0:T(1024)}, bf16[4096,128]{1,0:T(8,128)(2,1)}, /*index=5*/bf16[...) while((s32[]{:T(128)}, f32[8192,128]{1,0:T(8,128)}, ...), condition=%wide.region_4.5_spmd.clone, body=%wide.region_3.4_spmd.clone.sunk | while | flops 3256950784 | bytes 122636600 | solution.py:85
  173.0 7.0 mul.134
  180.9 19.6 %fusion.39 = bf16[512,8192]{1,0:T(8,128)(2,1)} fusion(f32[64,8,64,128]{3,2,1,0:T(8,128)} %bitcast.51, bf16[8192,128]{1,0:T(8,128)(2,1)S(1)} %copy-done.3, s32[8192]{0:T(1024)S(1)} %iota_add_fusion.3, f32[512]{0:T(512)S(1)} %dynamic_slice.59, f32[512]{0:T(512)S(1)} %dynamic_slice.60, s32[512]{0:T(512)S(1)} %dynamic_slice.61, ...), kind=kOutput, calls=%fused_computation.8.clone.1 | convolution fusion | flops 1107296256 | bytes 27432964 | tf_op jit(solution)/shard_map/while/body/eval_jaxpr/dot_general | solution.py:63
  200.6 7.9 %convolution_add_fusion.2 = f32[8192,128]{1,0:T(8,128)} fusion(bf16[512,8192]{1,0:T(8,128)(2,1)} %fusion.39, f32[8192,128]{1,0:T(8,128)} %get-tuple-element.310, pred[]{:T(512)S(6)} %compare.5, bf16[4096,128]{1,0:T(8,128)(2,1)} %get-tuple-element.327, s32[]{:T(128)S(6)} %select_n.53), kind=kOutput, calls=%fused_computation.9.clone.1 | convolution fusion | flops 1075838976 | bytes 16908292 | tf_op jit(solution)/shard_map/while/body/eval_jaxpr/dot_general | solution.py:76
  220.5 19.6 %fusion.39 = bf16[512,8192]{1,0:T(8,128)(2,1)} fusion(f32[64,8,64,128]{3,2,1,0:T(8,128)} %bitcast.51, bf16[8192,128]{1,0:T(8,128)(2,1)S(1)} %copy-done.3, s32[8192]{0:T(1024)S(1)} %iota_add_fusion.3, f32[512]{0:T(512)S(1)} %dynamic_slice.59, f32[512]{0:T(512)S(1)} %dynamic_slice.60, s32[512]{0:T(512)S(1)} %dynamic_slice.61, ...), kind=kOutput, calls=%fused_computation.8.clone.1 | convolution fusion | flops 1107296256 | bytes 27432964 | tf_op jit(solution)/shard_map/while/body/eval_jaxpr/dot_general | solution.py:63
  240.2 9.2 %convolution_add_fusion.2 = f32[8192,128]{1,0:T(8,128)} fusion(bf16[512,8192]{1,0:T(8,128)(2,1)} %fusion.39, f32[8192,128]{1,0:T(8,128)} %get-tuple-element.310, pred[]{:T(512)S(6)} %compare.5, bf16[4096,128]{1,0:T(8,128)(2,1)} %get-tuple-element.327, s32[]{:T(128)S(6)} %select_n.53), kind=kOutput, calls=%fused_computation.9.clone.1 | convolution fusion | flops 1075838976 | bytes 16908292 | tf_op jit(solution)/shard_map/while/body/eval_jaxpr/dot_general | solution.py:76
  253.4 7.0 mul.134
  261.3 19.7 %fusion.39 = bf16[512,8192]{1,0:T(8,128)(2,1)} fusion(f32[64,8,64,128]{3,2,1,0:T(8,128)} %bitcast.51, bf16[8192,128]{1,0:T(8,128)(2,1)S(1)} %copy-done.3, s32[8192]{0:T(1024)S(1)} %iota_add_fusion.3, f32[512]{0:T(512)S(1)} %dynamic_slice.59, f32[512]{0:T(512)S(1)} %dynamic_slice.60, s32[512]{0:T(512)S(1)} %dynamic_slice.61, ...), kind=kOutput, calls=%fused_computation.8.clone.1 | convolution fusion | flops 1107296256 | bytes 27432964 | tf_op jit(solution)/shard_map/while/body/eval_jaxpr/dot_general | solution.py:63
  281.0 9.2 %convolution_add_fusion.2 = f32[8192,128]{1,0:T(8,128)} fusion(bf16[512,8192]{1,0:T(8,128)(2,1)} %fusion.39, f32[8192,128]{1,0:T(8,128)} %get-tuple-element.310, pred[]{:T(512)S(6)} %compare.5, bf16[4096,128]{1,0:T(8,128)(2,1)} %get-tuple-element.327, s32[]{:T(128)S(6)} %select_n.53), kind=kOutput, calls=%fused_computation.9.clone.1 | convolution fusion | flops 1075838976 | bytes 16908292 | tf_op jit(solution)/shard_map/while/body/eval_jaxpr/dot_general | solution.py:76
  294.2 7.0 mul.134
  302.2 19.6 %fusion.39 = bf16[512,8192]{1,0:T(8,128)(2,1)} fusion(f32[64,8,64,128]{3,2,1,0:T(8,128)} %bitcast.51, bf16[8192,128]{1,0:T(8,128)(2,1)S(1)} %copy-done.3, s32[8192]{0:T(1024)S(1)} %iota_add_fusion.3, f32[512]{0:T(512)S(1)} %dynamic_slice.59, f32[512]{0:T(512)S(1)} %dynamic_slice.60, s32[512]{0:T(512)S(1)} %dynamic_slice.61, ...), kind=kOutput, calls=%fused_computation.8.clone.1 | convolution fusion | flops 1107296256 | bytes 27432964 | tf_op jit(solution)/shard_map/while/body/eval_jaxpr/dot_general | solution.py:63
  321.8 9.2 %convolution_add_fusion.2 = f32[8192,128]{1,0:T(8,128)} fusion(bf16[512,8192]{1,0:T(8,128)(2,1)} %fusion.39, f32[8192,128]{1,0:T(8,128)} %get-tuple-element.310, pred[]{:T(512)S(6)} %compare.5, bf16[4096,128]{1,0:T(8,128)(2,1)} %get-tuple-element.327, s32[]{:T(128)S(6)} %select_n.53), kind=kOutput, calls=%fused_computation.9.clone.1 | convolution fusion | flops 1075838976 | bytes 16908292 | tf_op jit(solution)/shard_map/while/body/eval_jaxpr/dot_general | solution.py:76
  335.0 7.0 mul.134
  343.0 19.6 %fusion.39 = bf16[512,8192]{1,0:T(8,128)(2,1)} fusion(f32[64,8,64,128]{3,2,1,0:T(8,128)} %bitcast.51, bf16[8192,128]{1,0:T(8,128)(2,1)S(1)} %copy-done.3, s32[8192]{0:T(1024)S(1)} %iota_add_fusion.3, f32[512]{0:T(512)S(1)} %dynamic_slice.59, f32[512]{0:T(512)S(1)} %dynamic_slice.60, s32[512]{0:T(512)S(1)} %dynamic_slice.61, ...), kind=kOutput, calls=%fused_computation.8.clone.1 | convolution fusion | flops 1107296256 | bytes 27432964 | tf_op jit(solution)/shard_map/while/body/eval_jaxpr/dot_general | solution.py:63
  362.6 9.2 %convolution_add_fusion.2 = f32[8192,128]{1,0:T(8,128)} fusion(bf16[512,8192]{1,0:T(8,128)(2,1)} %fusion.39, f32[8192,128]{1,0:T(8,128)} %get-tuple-element.310, pred[]{:T(512)S(6)} %compare.5, bf16[4096,128]{1,0:T(8,128)(2,1)} %get-tuple-element.327, s32[]{:T(128)S(6)} %select_n.53), kind=kOutput, calls=%fused_computation.9.clone.1 | convolution fusion | flops 1075838976 | bytes 16908292 | tf_op jit(solution)/shard_map/while/body/eval_jaxpr/dot_general | solution.py:76
  375.8 7.0 mul.134
  383.8 19.6 %fusion.39 = bf16[512,8192]{1,0:T(8,128)(2,1)} fusion(f32[64,8,64,128]{3,2,1,0:T(8,128)} %bitcast.51, bf16[8192,128]{1,0:T(8,128)(2,1)S(1)} %copy-done.3, s32[8192]{0:T(1024)S(1)} %iota_add_fusion.3, f32[512]{0:T(512)S(1)} %dynamic_slice.59, f32[512]{0:T(512)S(1)} %dynamic_slice.60, s32[512]{0:T(512)S(1)} %dynamic_slice.61, ...), kind=kOutput, calls=%fused_computation.8.clone.1 | convolution fusion | flops 1107296256 | bytes 27432964 | tf_op jit(solution)/shard_map/while/body/eval_jaxpr/dot_general | solution.py:63
  403.4 9.2 %convolution_add_fusion.2 = f32[8192,128]{1,0:T(8,128)} fusion(bf16[512,8192]{1,0:T(8,128)(2,1)} %fusion.39, f32[8192,128]{1,0:T(8,128)} %get-tuple-element.310, pred[]{:T(512)S(6)} %compare.5, bf16[4096,128]{1,0:T(8,128)(2,1)} %get-tuple-element.327, s32[]{:T(128)S(6)} %select_n.53), kind=kOutput, calls=%fused_computation.9.clone.1 | convolution fusion | flops 1075838976 | bytes 16908292 | tf_op jit(solution)/shard_map/while/body/eval_jaxpr/dot_general | solution.py:76
  416.6 7.0 mul.134
  424.5 19.6 %fusion.39 = bf16[512,8192]{1,0:T(8,128)(2,1)} fusion(f32[64,8,64,128]{3,2,1,0:T(8,128)} %bitcast.51, bf16[8192,128]{1,0:T(8,128)(2,1)S(1)} %copy-done.3, s32[8192]{0:T(1024)S(1)} %iota_add_fusion.3, f32[512]{0:T(512)S(1)} %dynamic_slice.59, f32[512]{0:T(512)S(1)} %dynamic_slice.60, s32[512]{0:T(512)S(1)} %dynamic_slice.61, ...), kind=kOutput, calls=%fused_computation.8.clone.1 | convolution fusion | flops 1107296256 | bytes 27432964 | tf_op jit(solution)/shard_map/while/body/eval_jaxpr/dot_general | solution.py:63
  444.2 9.2 %convolution_add_fusion.2 = f32[8192,128]{1,0:T(8,128)} fusion(bf16[512,8192]{1,0:T(8,128)(2,1)} %fusion.39, f32[8192,128]{1,0:T(8,128)} %get-tuple-element.310, pred[]{:T(512)S(6)} %compare.5, bf16[4096,128]{1,0:T(8,128)(2,1)} %get-tuple-element.327, s32[]{:T(128)S(6)} %select_n.53), kind=kOutput, calls=%fused_computation.9.clone.1 | convolution fusion | flops 1075838976 | bytes 16908292 | tf_op jit(solution)/shard_map/while/body/eval_jaxpr/dot_general | solution.py:76
  465.3 19.6 %fusion.39 = bf16[512,8192]{1,0:T(8,128)(2,1)} fusion(f32[64,8,64,128]{3,2,1,0:T(8,128)} %bitcast.51, bf16[8192,128]{1,0:T(8,128)(2,1)S(1)} %copy-done.3, s32[8192]{0:T(1024)S(1)} %iota_add_fusion.3, f32[512]{0:T(512)S(1)} %dynamic_slice.59, f32[512]{0:T(512)S(1)} %dynamic_slice.60, s32[512]{0:T(512)S(1)} %dynamic_slice.61, ...), kind=kOutput, calls=%fused_computation.8.clone.1 | convolution fusion | flops 1107296256 | bytes 27432964 | tf_op jit(solution)/shard_map/while/body/eval_jaxpr/dot_general | solution.py:63
  485.0 9.2 %convolution_add_fusion.2 = f32[8192,128]{1,0:T(8,128)} fusion(bf16[512,8192]{1,0:T(8,128)(2,1)} %fusion.39, f32[8192,128]{1,0:T(8,128)} %get-tuple-element.310, pred[]{:T(512)S(6)} %compare.5, bf16[4096,128]{1,0:T(8,128)(2,1)} %get-tuple-element.327, s32[]{:T(128)S(6)} %select_n.53), kind=kOutput, calls=%fused_computation.9.clone.1 | convolution fusion | flops 1075838976 | bytes 16908292 | tf_op jit(solution)/shard_map/while/body/eval_jaxpr/dot_general | solution.py:76
  505.0 8.7 %scatter_fusion = bf16[256,128,128]{2,1,0:T(8,128)(2,1)} fusion(bf16[256,128,128]{2,1,0:T(8,128)(2,1)} %broadcast_in_dim.74, s32[64]{0:T(128)S(1)} %bitcast.56, bf16[64,128,128]{2,1,0:T(8,128)(2,1)S(1)} %bitcast.52), kind=kCustom, calls=%fused_computation.3 | custom fusion | bytes 6291712 | tf_op jit(solution)/shard_map/scatter | solution.py:89
  513.8 11.4 %all-to-all-start.2 = ((bf16[256,128,128]{2,1,0:T(8,128)(2,1)}), bf16[256,128,128]{2,1,0:T(8,128)(2,1)}, u32[]{:S(2)}, u32[]{:S(2)}) async-start(bf16[256,128,128]{2,1,0:T(8,128)(2,1)} %scatter_fusion), calls=%async_computation.2 | async-start | bytes 16777216 | tf_op jit(solution)/shard_map/all_to_all | solution.py:90
  526.0 173.4 %all-reduce.2.cloned.1.call-done = f32[4096,128]{1,0:T(8,128)} async-done(((f32[4096,128]{1,0:T(8,128)}), f32[4096,128]{1,0:T(8,128)}) %all-reduce.2.cloned.1.call-update) | async-done | bytes 2097168 | tf_op jit(solution)/shard_map/psum | solution.py:99
  701.0 10.5 %fusion.10 = f32[64,16384]{1,0:T(8,128)} fusion(bf16[32,8,128,128]{3,2,1,0:T(8,128)(2,1)} %bitcast.12, s32[256]{0:T(256)S(1)} %copy-done.9), kind=kOutput, calls=%fused_computation.18 | convolution fusion | flops 536887296 | bytes 12583936 | tf_op jit(solution)/shard_map/dot_general | solution.py:94
  (143 shorter events, 93.5 us)
Async XLA Ops:
  7.2 25.1 %copy-start = (bf16[8192,128]{1,0:T(8,128)(2,1)S(1)}, bf16[8192,128]{1,0:T(8,128)(2,1)}, u32[]{:S(2)}) copy-start(bf16[8192,128]{1,0:T(8,128)(2,1)} %param.11) | copy-start | bytes 6291460
  32.0 8.5 %copy-start.8 = (s32[256]{0:T(256)}, s32[256]{0:T(256)S(1)}, u32[]{:S(2)}) copy-start(s32[256]{0:T(256)S(1)} %all_to_all.16) | copy-start | bytes 3076
  48.0 9.5 %copy-start.7 = (f32[4096]{0:T(1024)S(1)}, f32[4096]{0:T(1024)}, u32[]{:S(2)}) copy-start(f32[4096]{0:T(1024)} %param.12) | copy-start | bytes 49156
  48.0 104.9 %all-to-all-start.1 = ((bf16[256,128,128]{2,1,0:T(8,128)(2,1)}), bf16[256,128,128]{2,1,0:T(8,128)(2,1)}, u32[]{:S(2)}, u32[]{:S(2)}) async-start(bf16[256,128,128]{2,1,0:T(8,128)(2,1)} %broadcast_select_fusion), calls=%async_computation.1 | async-start | bytes 16777216 | tf_op jit(solution)/shard_map/all_to_all | solution.py:38
  54.1 116.5 %all-gather.2.cloned.1.call-start = ((), (), s32[]{:S(2)}) async-start(), calls=%async_computation.3 | async-start | bytes 1114112 | tf_op jit(solution)/shard_map/all_gather | solution.py:31
  173.0 8.0 %copy-start.3 = (bf16[8192,128]{1,0:T(8,128)(2,1)S(1)}, bf16[8192,128]{1,0:T(8,128)(2,1)}, u32[]{:S(2)}) copy-start(bf16[8192,128]{1,0:T(8,128)(2,1)} %get-tuple-element.328) | copy-start | bytes 6291460 | tf_op jit(solution)/shard_map/while
  200.6 7.9 %copy-start.4 = (bf16[8192,128]{1,0:T(8,128)(2,1)S(1)}, bf16[8192,128]{1,0:T(8,128)(2,1)}, u32[]{:S(2)}) copy-start(bf16[8192,128]{1,0:T(8,128)(2,1)} %get-tuple-element.328) | copy-start | bytes 6291460 | tf_op jit(solution)/shard_map/while
  212.6 8.0 %copy-start.3 = (bf16[8192,128]{1,0:T(8,128)(2,1)S(1)}, bf16[8192,128]{1,0:T(8,128)(2,1)}, u32[]{:S(2)}) copy-start(bf16[8192,128]{1,0:T(8,128)(2,1)} %get-tuple-element.328) | copy-start | bytes 6291460 | tf_op jit(solution)/shard_map/while
  240.2 9.2 %copy-start.2 = (bf16[512,8192]{1,0:T(8,128)(2,1)S(1)}, bf16[512,8192]{1,0:T(8,128)(2,1)}, u32[]{:S(2)}) copy-start(bf16[512,8192]{1,0:T(8,128)(2,1)} %fusion.39) | copy-start | bytes 25165828 | tf_op jit(solution)/shard_map/while
  240.2 9.2 %copy-start.4 = (bf16[8192,128]{1,0:T(8,128)(2,1)S(1)}, bf16[8192,128]{1,0:T(8,128)(2,1)}, u32[]{:S(2)}) copy-start(bf16[8192,128]{1,0:T(8,128)(2,1)} %get-tuple-element.328) | copy-start | bytes 6291460 | tf_op jit(solution)/shard_map/while
  253.4 8.0 %copy-start.3 = (bf16[8192,128]{1,0:T(8,128)(2,1)S(1)}, bf16[8192,128]{1,0:T(8,128)(2,1)}, u32[]{:S(2)}) copy-start(bf16[8192,128]{1,0:T(8,128)(2,1)} %get-tuple-element.328) | copy-start | bytes 6291460 | tf_op jit(solution)/shard_map/while
  281.0 9.2 %copy-start.2 = (bf16[512,8192]{1,0:T(8,128)(2,1)S(1)}, bf16[512,8192]{1,0:T(8,128)(2,1)}, u32[]{:S(2)}) copy-start(bf16[512,8192]{1,0:T(8,128)(2,1)} %fusion.39) | copy-start | bytes 25165828 | tf_op jit(solution)/shard_map/while
  281.0 9.2 %copy-start.4 = (bf16[8192,128]{1,0:T(8,128)(2,1)S(1)}, bf16[8192,128]{1,0:T(8,128)(2,1)}, u32[]{:S(2)}) copy-start(bf16[8192,128]{1,0:T(8,128)(2,1)} %get-tuple-element.328) | copy-start | bytes 6291460 | tf_op jit(solution)/shard_map/while
  294.2 8.0 %copy-start.3 = (bf16[8192,128]{1,0:T(8,128)(2,1)S(1)}, bf16[8192,128]{1,0:T(8,128)(2,1)}, u32[]{:S(2)}) copy-start(bf16[8192,128]{1,0:T(8,128)(2,1)} %get-tuple-element.328) | copy-start | bytes 6291460 | tf_op jit(solution)/shard_map/while
  321.8 9.2 %copy-start.2 = (bf16[512,8192]{1,0:T(8,128)(2,1)S(1)}, bf16[512,8192]{1,0:T(8,128)(2,1)}, u32[]{:S(2)}) copy-start(bf16[512,8192]{1,0:T(8,128)(2,1)} %fusion.39) | copy-start | bytes 25165828 | tf_op jit(solution)/shard_map/while
  321.8 9.2 %copy-start.4 = (bf16[8192,128]{1,0:T(8,128)(2,1)S(1)}, bf16[8192,128]{1,0:T(8,128)(2,1)}, u32[]{:S(2)}) copy-start(bf16[8192,128]{1,0:T(8,128)(2,1)} %get-tuple-element.328) | copy-start | bytes 6291460 | tf_op jit(solution)/shard_map/while
  335.0 8.0 %copy-start.3 = (bf16[8192,128]{1,0:T(8,128)(2,1)S(1)}, bf16[8192,128]{1,0:T(8,128)(2,1)}, u32[]{:S(2)}) copy-start(bf16[8192,128]{1,0:T(8,128)(2,1)} %get-tuple-element.328) | copy-start | bytes 6291460 | tf_op jit(solution)/shard_map/while
  362.6 9.2 %copy-start.2 = (bf16[512,8192]{1,0:T(8,128)(2,1)S(1)}, bf16[512,8192]{1,0:T(8,128)(2,1)}, u32[]{:S(2)}) copy-start(bf16[512,8192]{1,0:T(8,128)(2,1)} %fusion.39) | copy-start | bytes 25165828 | tf_op jit(solution)/shard_map/while
  362.6 9.2 %copy-start.4 = (bf16[8192,128]{1,0:T(8,128)(2,1)S(1)}, bf16[8192,128]{1,0:T(8,128)(2,1)}, u32[]{:S(2)}) copy-start(bf16[8192,128]{1,0:T(8,128)(2,1)} %get-tuple-element.328) | copy-start | bytes 6291460 | tf_op jit(solution)/shard_map/while
  375.8 8.0 %copy-start.3 = (bf16[8192,128]{1,0:T(8,128)(2,1)S(1)}, bf16[8192,128]{1,0:T(8,128)(2,1)}, u32[]{:S(2)}) copy-start(bf16[8192,128]{1,0:T(8,128)(2,1)} %get-tuple-element.328) | copy-start | bytes 6291460 | tf_op jit(solution)/shard_map/while
  403.4 9.2 %copy-start.2 = (bf16[512,8192]{1,0:T(8,128)(2,1)S(1)}, bf16[512,8192]{1,0:T(8,128)(2,1)}, u32[]{:S(2)}) copy-start(bf16[512,8192]{1,0:T(8,128)(2,1)} %fusion.39) | copy-start | bytes 25165828 | tf_op jit(solution)/shard_map/while
  403.4 9.2 %copy-start.4 = (bf16[8192,128]{1,0:T(8,128)(2,1)S(1)}, bf16[8192,128]{1,0:T(8,128)(2,1)}, u32[]{:S(2)}) copy-start(bf16[8192,128]{1,0:T(8,128)(2,1)} %get-tuple-element.328) | copy-start | bytes 6291460 | tf_op jit(solution)/shard_map/while
  416.6 8.0 %copy-start.3 = (bf16[8192,128]{1,0:T(8,128)(2,1)S(1)}, bf16[8192,128]{1,0:T(8,128)(2,1)}, u32[]{:S(2)}) copy-start(bf16[8192,128]{1,0:T(8,128)(2,1)} %get-tuple-element.328) | copy-start | bytes 6291460 | tf_op jit(solution)/shard_map/while
  444.2 9.2 %copy-start.2 = (bf16[512,8192]{1,0:T(8,128)(2,1)S(1)}, bf16[512,8192]{1,0:T(8,128)(2,1)}, u32[]{:S(2)}) copy-start(bf16[512,8192]{1,0:T(8,128)(2,1)} %fusion.39) | copy-start | bytes 25165828 | tf_op jit(solution)/shard_map/while
  444.2 9.2 %copy-start.4 = (bf16[8192,128]{1,0:T(8,128)(2,1)S(1)}, bf16[8192,128]{1,0:T(8,128)(2,1)}, u32[]{:S(2)}) copy-start(bf16[8192,128]{1,0:T(8,128)(2,1)} %get-tuple-element.328) | copy-start | bytes 6291460 | tf_op jit(solution)/shard_map/while
  457.4 8.0 %copy-start.3 = (bf16[8192,128]{1,0:T(8,128)(2,1)S(1)}, bf16[8192,128]{1,0:T(8,128)(2,1)}, u32[]{:S(2)}) copy-start(bf16[8192,128]{1,0:T(8,128)(2,1)} %get-tuple-element.328) | copy-start | bytes 6291460 | tf_op jit(solution)/shard_map/while
  485.0 9.2 %copy-start.2 = (bf16[512,8192]{1,0:T(8,128)(2,1)S(1)}, bf16[512,8192]{1,0:T(8,128)(2,1)}, u32[]{:S(2)}) copy-start(bf16[512,8192]{1,0:T(8,128)(2,1)} %fusion.39) | copy-start | bytes 25165828 | tf_op jit(solution)/shard_map/while
  485.0 9.2 %copy-start.4 = (bf16[8192,128]{1,0:T(8,128)(2,1)S(1)}, bf16[8192,128]{1,0:T(8,128)(2,1)}, u32[]{:S(2)}) copy-start(bf16[8192,128]{1,0:T(8,128)(2,1)} %get-tuple-element.328) | copy-start | bytes 6291460 | tf_op jit(solution)/shard_map/while
  513.8 187.2 %copy-start.9 = (s32[256]{0:T(256)S(1)}, s32[256]{0:T(256)}, u32[]{:S(2)}) copy-start(s32[256]{0:T(256)} %copy-done.8) | copy-start | bytes 3076
  513.8 187.2 %all-to-all-start.2 = ((bf16[256,128,128]{2,1,0:T(8,128)(2,1)}), bf16[256,128,128]{2,1,0:T(8,128)(2,1)}, u32[]{:S(2)}, u32[]{:S(2)}) async-start(bf16[256,128,128]{2,1,0:T(8,128)(2,1)} %scatter_fusion), calls=%async_computation.2 | async-start | bytes 16777216 | tf_op jit(solution)/shard_map/all_to_all | solution.py:90
  525.2 174.2 %all-reduce.2.cloned.1.call-start = ((), (), s32[]{:S(2)}) async-start(), calls=%async_computation.4 | async-start | bytes 4194304 | tf_op jit(solution)/shard_map/psum | solution.py:99
  701.0 15.4 %copy-start.1 = (bf16[8192,128]{1,0:T(8,128)(2,1)S(1)}, bf16[8192,128]{1,0:T(8,128)(2,1)}, u32[]{:S(2)}) copy-start(bf16[8192,128]{1,0:T(8,128)(2,1)} %param.11) | copy-start | bytes 6291460
  (3 other events, 22.4 us)
Sparse Core Ops, SparseCore 0:
  57.0 113.4 all-gather.1
  529.4 169.9 all-reduce.1
where the time goes:
time: 725 us; the launch traced here: 723 us
  waiting for transfers between devices  278 us (38%)
  matrix products  264 us (36%)
  local copies, waits for them, and re-layouts  108 us (15%)
  blocking collectives  20.5 us (3%)
  other arithmetic  20.2 us (3%)
  starting transfers between devices  17.6 us (2%)
  between operations  14.2 us (2%)
    psum x1, waiting for transfers between devices, shards(): summed = lax.psum(query_grad, 'narrow')  173 us
    dot_general x8, matrix products, one_block(): lax.dot_general(query_block, fetched, (((1,), (1,)), ((), ())), preferred...  157 us
    all_to_all x1, waiting for transfers between devices, shards(): lax.all_to_all(served, ('wide', 'narrow'), split_axis=0, concat_axis=0, t...  95.4 us
    dot_general x8, matrix products, one_block(): lax.dot_general(logit_grad, query_block, (((0,), (0,)), ((), ())), prefer...  72 us
    mul x8, local copies, waits for them, and re-layouts, one_block(): softmax_terms.reshape(block_size, fetch_count, BLOCK)  56.3 us
    dot_general x8, matrix products, one_block(): jnp.dot(logit_grad, fetched, preferred_element_type=jnp.float32)  24.5 us
    all_to_all x1, blocking collectives, shards(): lax.all_to_all(requests, ('wide', 'narrow'), split_axis=0, concat_axis=0,...  20.5 us
  transfers between devices with their start and end apart: 4, of which 3 were waited for; matrix products, arithmetic and copies ran while one was open for 2% of the time, Pallas kernels for 0%

commit v1 on v0

--- a/solution.py
+++ b/solution.py
@@ -96,7 +96,9 @@
     )
     index_grad = index_grad.reshape(blocks_here * BLOCK, feat_width)
     own_rows = queries.shape[0]
-    summed = lax.psum(query_grad, "narrow")
+    summed = query_grad
+    for hop in (1, 2, 4, 8):
+        summed = summed + lax.ppermute(summed, "narrow", [(dev, dev ^ hop) for dev in range(16)])
     query_out = lax.dynamic_slice_in_dim(summed, narrow_pos * own_rows, own_rows, 0)
     return (query_out, index_grad)
 

time: 725 us -> 829 us (1.14)
  waiting for transfers between devices: 278 us -> 361 us
  starting transfers between devices: 17.6 us -> 29.7 us
    ppermute x0 -> x4, waiting for transfers between devices: none -> 257 us  [shards(): lax.ppermute(summed, 'narrow', [(dev, dev ^ hop) for dev in range(16)])]
    psum x1 -> x0, waiting for transfers between devices: 173 us -> none  [shards(): summed = lax.psum(query_grad, 'narrow')]
    ppermute x0 -> x4, starting transfers between devices: none -> 12.3 us  [shards(): lax.ppermute(summed, 'narrow', [(dev, dev ^ hop) for dev in range(16)])]
  transfers between devices with their start and end apart: 4 -> 7, of which waited for: 3 -> 6; matrix products, arithmetic and copies ran while one was open for 2% -> 4% of each run, Pallas kernels for 0% -> 0%
where the time goes in v1:
time: 829 us; the launch traced here: 821 us
  waiting for transfers between devices  361 us (44%)
  matrix products  263 us (32%)
  local copies, waits for them, and re-layouts  106 us (13%)
  starting transfers between devices  29.7 us (4%)
  other arithmetic  25.7 us (3%)
  blocking collectives  20.5 us (2%)
  between operations  14.2 us (2%)
    ppermute x4, waiting for transfers between devices, shards(): lax.ppermute(summed, 'narrow', [(dev, dev ^ hop) for dev in range(16)])  257 us
    dot_general x8, matrix products, one_block(): lax.dot_general(query_block, fetched, (((1,), (1,)), ((), ())), preferred...  156 us
    all_to_all x1, waiting for transfers between devices, shards(): lax.all_to_all(served, ('wide', 'narrow'), split_axis=0, concat_axis=0, t...  95.4 us
    dot_general x8, matrix products, one_block(): lax.dot_general(logit_grad, query_block, (((0,), (0,)), ((), ())), prefer...  72.1 us
    mul x8, local copies, waits for them, and re-layouts, one_block(): softmax_terms.reshape(block_size, fetch_count, BLOCK)  56.2 us
    dot_general x8, matrix products, one_block(): jnp.dot(logit_grad, fetched, preferred_element_type=jnp.float32)  24.4 us
    all_to_all x1, blocking collectives, shards(): lax.all_to_all(requests, ('wide', 'narrow'), split_axis=0, concat_axis=0,...  20.5 us
  transfers between devices with their start and end apart: 7, of which 6 were waited for; matrix products, arithmetic and copies ran while one was open for 4% of the time, Pallas kernels for 0%

profile of v1, /device:TPU:0, one launch (start us, length us, event | category | flops | bytes accessed | tf_op | source)
XLA Modules:
  0.0 820.8 jit_solution(13295465477594225531)
XLA Ops:
  9.9 20.5 %all_to_all.22 = s32[128,2,1]{1,2,0:T(1,128)S(1)} all-to-all(s32[128,2,1]{1,2,0:T(1,128)S(1)} %bitcast.53), channel_id=1, replica_groups=mesh['wide'=8,'narrow'=16] {'wide','narrow'}, dimensions={0} | all-to-all | bytes 2048 | tf_op jit(solution)/shard_map/all_to_all | solution.py:33
  32.2 8.4 %gather_fusion = bf16[256,128,128]{2,1,0:T(8,128)(2,1)} fusion(bf16[64,128,128]{2,1,0:T(8,128)(2,1)S(1)} %bitcast.50, s32[1024]{0:T(1024)S(1)} %pad_clamp_fusion.1), kind=kCustom, calls=%fused_computation | custom fusion | bytes 16778240 | tf_op jit(solution)/shard_map/jit(_take)/gather | solution.py:37
  40.6 7.4 broadcast_select_fusion
  57.5 95.4 %all-to-all-done.1 = bf16[256,128,128]{2,1,0:T(8,128)(2,1)} async-done(((bf16[256,128,128]{2,1,0:T(8,128)(2,1)}), bf16[256,128,128]{2,1,0:T(8,128)(2,1)}, u32[]{:S(2)}, u32[]{:S(2)}) %all-to-all-start.1) | async-done | bytes 8388640 | tf_op jit(solution)/shard_map/all_to_all | solution.py:38
  162.3 8.2 %all-gather.2.cloned.1.call-done = bf16[4096,128]{1,0:T(8,128)(2,1)} async-done(((bf16[256,128]{1,0:T(8,128)(2,1)}), bf16[4096,128]{1,0:T(8,128)(2,1)}) %all-gather.2.cloned.1.call-update) | async-done | bytes 1048592 | tf_op jit(solution)/shard_map/all_gather | solution.py:31
  172.0 324.1 %while.16 = (s32[]{:T(128)}, f32[8192,128]{1,0:T(8,128)}, f32[4096,128]{1,0:T(8,128)}, f32[4096]{0:T(1024)}, bf16[4096,128]{1,0:T(8,128)(2,1)}, /*index=5*/bf16[...) while((s32[]{:T(128)}, f32[8192,128]{1,0:T(8,128)}, ...), condition=%wide.region_4.5_spmd.clone, body=%wide.region_3.4_spmd.clone.sunk | while | flops 3256950784 | bytes 122636600 | solution.py:85
  173.0 7.0 mul.134
  181.0 19.5 %fusion.39 = bf16[512,8192]{1,0:T(8,128)(2,1)} fusion(f32[64,8,64,128]{3,2,1,0:T(8,128)} %bitcast.51, bf16[8192,128]{1,0:T(8,128)(2,1)S(1)} %copy-done.4, s32[8192]{0:T(1024)S(1)} %iota_add_fusion.3, f32[512]{0:T(512)S(1)} %dynamic_slice.62, f32[512]{0:T(512)S(1)} %dynamic_slice.63, s32[512]{0:T(512)S(1)} %dynamic_slice.64, ...), kind=kOutput, calls=%fused_computation.8.clone.1 | convolution fusion | flops 1107296256 | bytes 27432964 | tf_op jit(solution)/shard_map/while/body/eval_jaxpr/dot_general | solution.py:63
  200.5 7.9 convolution_add_fusion.2
  212.5 7.0 mul.134
  220.4 19.5 %fusion.39 = bf16[512,8192]{1,0:T(8,128)(2,1)} fusion(f32[64,8,64,128]{3,2,1,0:T(8,128)} %bitcast.51, bf16[8192,128]{1,0:T(8,128)(2,1)S(1)} %copy-done.4, s32[8192]{0:T(1024)S(1)} %iota_add_fusion.3, f32[512]{0:T(512)S(1)} %dynamic_slice.62, f32[512]{0:T(512)S(1)} %dynamic_slice.63, s32[512]{0:T(512)S(1)} %dynamic_slice.64, ...), kind=kOutput, calls=%fused_computation.8.clone.1 | convolution fusion | flops 1107296256 | bytes 27432964 | tf_op jit(solution)/shard_map/while/body/eval_jaxpr/dot_general | solution.py:63
  239.9 9.2 %convolution_add_fusion.2 = f32[8192,128]{1,0:T(8,128)} fusion(bf16[512,8192]{1,0:T(8,128)(2,1)} %fusion.39, f32[8192,128]{1,0:T(8,128)} %get-tuple-element.310, pred[]{:T(512)S(6)} %compare.5, bf16[4096,128]{1,0:T(8,128)(2,1)} %get-tuple-element.327, s32[]{:T(128)S(6)} %select_n.53), kind=kOutput, calls=%fused_computation.9.clone.1 | convolution fusion | flops 1075838976 | bytes 16908292 | tf_op jit(solution)/shard_map/while/body/eval_jaxpr/dot_general | solution.py:76
  261.1 19.5 %fusion.39 = bf16[512,8192]{1,0:T(8,128)(2,1)} fusion(f32[64,8,64,128]{3,2,1,0:T(8,128)} %bitcast.51, bf16[8192,128]{1,0:T(8,128)(2,1)S(1)} %copy-done.4, s32[8192]{0:T(1024)S(1)} %iota_add_fusion.3, f32[512]{0:T(512)S(1)} %dynamic_slice.62, f32[512]{0:T(512)S(1)} %dynamic_slice.63, s32[512]{0:T(512)S(1)} %dynamic_slice.64, ...), kind=kOutput, calls=%fused_computation.8.clone.1 | convolution fusion | flops 1107296256 | bytes 27432964 | tf_op jit(solution)/shard_map/while/body/eval_jaxpr/dot_general | solution.py:63
  280.6 9.2 %convolution_add_fusion.2 = f32[8192,128]{1,0:T(8,128)} fusion(bf16[512,8192]{1,0:T(8,128)(2,1)} %fusion.39, f32[8192,128]{1,0:T(8,128)} %get-tuple-element.310, pred[]{:T(512)S(6)} %compare.5, bf16[4096,128]{1,0:T(8,128)(2,1)} %get-tuple-element.327, s32[]{:T(128)S(6)} %select_n.53), kind=kOutput, calls=%fused_computation.9.clone.1 | convolution fusion | flops 1075838976 | bytes 16908292 | tf_op jit(solution)/shard_map/while/body/eval_jaxpr/dot_general | solution.py:76
  293.8 7.0 mul.134
  301.8 19.5 %fusion.39 = bf16[512,8192]{1,0:T(8,128)(2,1)} fusion(f32[64,8,64,128]{3,2,1,0:T(8,128)} %bitcast.51, bf16[8192,128]{1,0:T(8,128)(2,1)S(1)} %copy-done.4, s32[8192]{0:T(1024)S(1)} %iota_add_fusion.3, f32[512]{0:T(512)S(1)} %dynamic_slice.62, f32[512]{0:T(512)S(1)} %dynamic_slice.63, s32[512]{0:T(512)S(1)} %dynamic_slice.64, ...), kind=kOutput, calls=%fused_computation.8.clone.1 | convolution fusion | flops 1107296256 | bytes 27432964 | tf_op jit(solution)/shard_map/while/body/eval_jaxpr/dot_general | solution.py:63
  321.3 9.2 %convolution_add_fusion.2 = f32[8192,128]{1,0:T(8,128)} fusion(bf16[512,8192]{1,0:T(8,128)(2,1)} %fusion.39, f32[8192,128]{1,0:T(8,128)} %get-tuple-element.310, pred[]{:T(512)S(6)} %compare.5, bf16[4096,128]{1,0:T(8,128)(2,1)} %get-tuple-element.327, s32[]{:T(128)S(6)} %select_n.53), kind=kOutput, calls=%fused_computation.9.clone.1 | convolution fusion | flops 1075838976 | bytes 16908292 | tf_op jit(solution)/shard_map/while/body/eval_jaxpr/dot_general | solution.py:76
  342.4 19.5 %fusion.39 = bf16[512,8192]{1,0:T(8,128)(2,1)} fusion(f32[64,8,64,128]{3,2,1,0:T(8,128)} %bitcast.51, bf16[8192,128]{1,0:T(8,128)(2,1)S(1)} %copy-done.4, s32[8192]{0:T(1024)S(1)} %iota_add_fusion.3, f32[512]{0:T(512)S(1)} %dynamic_slice.62, f32[512]{0:T(512)S(1)} %dynamic_slice.63, s32[512]{0:T(512)S(1)} %dynamic_slice.64, ...), kind=kOutput, calls=%fused_computation.8.clone.1 | convolution fusion | flops 1107296256 | bytes 27432964 | tf_op jit(solution)/shard_map/while/body/eval_jaxpr/dot_general | solution.py:63
  361.9 9.2 %convolution_add_fusion.2 = f32[8192,128]{1,0:T(8,128)} fusion(bf16[512,8192]{1,0:T(8,128)(2,1)} %fusion.39, f32[8192,128]{1,0:T(8,128)} %get-tuple-element.310, pred[]{:T(512)S(6)} %compare.5, bf16[4096,128]{1,0:T(8,128)(2,1)} %get-tuple-element.327, s32[]{:T(128)S(6)} %select_n.53), kind=kOutput, calls=%fused_computation.9.clone.1 | convolution fusion | flops 1075838976 | bytes 16908292 | tf_op jit(solution)/shard_map/while/body/eval_jaxpr/dot_general | solution.py:76
  383.1 19.5 %fusion.39 = bf16[512,8192]{1,0:T(8,128)(2,1)} fusion(f32[64,8,64,128]{3,2,1,0:T(8,128)} %bitcast.51, bf16[8192,128]{1,0:T(8,128)(2,1)S(1)} %copy-done.4, s32[8192]{0:T(1024)S(1)} %iota_add_fusion.3, f32[512]{0:T(512)S(1)} %dynamic_slice.62, f32[512]{0:T(512)S(1)} %dynamic_slice.63, s32[512]{0:T(512)S(1)} %dynamic_slice.64, ...), kind=kOutput, calls=%fused_computation.8.clone.1 | convolution fusion | flops 1107296256 | bytes 27432964 | tf_op jit(solution)/shard_map/while/body/eval_jaxpr/dot_general | solution.py:63
  402.6 9.2 %convolution_add_fusion.2 = f32[8192,128]{1,0:T(8,128)} fusion(bf16[512,8192]{1,0:T(8,128)(2,1)} %fusion.39, f32[8192,128]{1,0:T(8,128)} %get-tuple-element.310, pred[]{:T(512)S(6)} %compare.5, bf16[4096,128]{1,0:T(8,128)(2,1)} %get-tuple-element.327, s32[]{:T(128)S(6)} %select_n.53), kind=kOutput, calls=%fused_computation.9.clone.1 | convolution fusion | flops 1075838976 | bytes 16908292 | tf_op jit(solution)/shard_map/while/body/eval_jaxpr/dot_general | solution.py:76
  423.8 19.5 %fusion.39 = bf16[512,8192]{1,0:T(8,128)(2,1)} fusion(f32[64,8,64,128]{3,2,1,0:T(8,128)} %bitcast.51, bf16[8192,128]{1,0:T(8,128)(2,1)S(1)} %copy-done.4, s32[8192]{0:T(1024)S(1)} %iota_add_fusion.3, f32[512]{0:T(512)S(1)} %dynamic_slice.62, f32[512]{0:T(512)S(1)} %dynamic_slice.63, s32[512]{0:T(512)S(1)} %dynamic_slice.64, ...), kind=kOutput, calls=%fused_computation.8.clone.1 | convolution fusion | flops 1107296256 | bytes 27432964 | tf_op jit(solution)/shard_map/while/body/eval_jaxpr/dot_general | solution.py:63
  443.3 9.2 %convolution_add_fusion.2 = f32[8192,128]{1,0:T(8,128)} fusion(bf16[512,8192]{1,0:T(8,128)(2,1)} %fusion.39, f32[8192,128]{1,0:T(8,128)} %get-tuple-element.310, pred[]{:T(512)S(6)} %compare.5, bf16[4096,128]{1,0:T(8,128)(2,1)} %get-tuple-element.327, s32[]{:T(128)S(6)} %select_n.53), kind=kOutput, calls=%fused_computation.9.clone.1 | convolution fusion | flops 1075838976 | bytes 16908292 | tf_op jit(solution)/shard_map/while/body/eval_jaxpr/dot_general | solution.py:76
  464.4 19.5 %fusion.39 = bf16[512,8192]{1,0:T(8,128)(2,1)} fusion(f32[64,8,64,128]{3,2,1,0:T(8,128)} %bitcast.51, bf16[8192,128]{1,0:T(8,128)(2,1)S(1)} %copy-done.4, s32[8192]{0:T(1024)S(1)} %iota_add_fusion.3, f32[512]{0:T(512)S(1)} %dynamic_slice.62, f32[512]{0:T(512)S(1)} %dynamic_slice.63, s32[512]{0:T(512)S(1)} %dynamic_slice.64, ...), kind=kOutput, calls=%fused_computation.8.clone.1 | convolution fusion | flops 1107296256 | bytes 27432964 | tf_op jit(solution)/shard_map/while/body/eval_jaxpr/dot_general | solution.py:63
  483.9 9.2 %convolution_add_fusion.2 = f32[8192,128]{1,0:T(8,128)} fusion(bf16[512,8192]{1,0:T(8,128)(2,1)} %fusion.39, f32[8192,128]{1,0:T(8,128)} %get-tuple-element.310, pred[]{:T(512)S(6)} %compare.5, bf16[4096,128]{1,0:T(8,128)(2,1)} %get-tuple-element.327, s32[]{:T(128)S(6)} %select_n.53), kind=kOutput, calls=%fused_computation.9.clone.1 | convolution fusion | flops 1075838976 | bytes 16908292 | tf_op jit(solution)/shard_map/while/body/eval_jaxpr/dot_general | solution.py:76
  504.0 8.6 %scatter_fusion = bf16[256,128,128]{2,1,0:T(8,128)(2,1)} fusion(bf16[256,128,128]{2,1,0:T(8,128)(2,1)} %broadcast_in_dim.74, s32[64]{0:T(128)S(1)} %bitcast.56, bf16[64,128,128]{2,1,0:T(8,128)(2,1)S(1)} %bitcast.52), kind=kCustom, calls=%fused_computation.3 | custom fusion | bytes 6291712 | tf_op jit(solution)/shard_map/scatter | solution.py:89
  512.6 11.4 %all-to-all-start.2 = ((bf16[256,128,128]{2,1,0:T(8,128)(2,1)}), bf16[256,128,128]{2,1,0:T(8,128)(2,1)}, u32[]{:S(2)}, u32[]{:S(2)}) async-start(bf16[256,128,128]{2,1,0:T(8,128)(2,1)} %scatter_fusion), calls=%async_computation.2 | async-start | bytes 16777216 | tf_op jit(solution)/shard_map/all_to_all | solution.py:90
  525.0 137.8 %collective-permute-done = f32[4096,128]{1,0:T(8,128)S(1)} collective-permute-done((f32[4096,128]{1,0:T(8,128)S(1)}, f32[4096,128]{1,0:T(8,128)S(1)}, u32[]{:S(2)}, u32[]{:S(2)}) %collective-permute-start) | collective-permute-done | bytes 2097184 | tf_op jit(solution)/shard_map/ppermute | solution.py:101
  668.2 45.3 %collective-permute-done.1 = f32[4096,128]{1,0:T(8,128)S(1)} collective-permute-done((f32[4096,128]{1,0:T(8,128)S(1)}, f32[4096,128]{1,0:T(8,128)S(1)}, u32[]{:S(2)}, u32[]{:S(2)}) %collective-permute-start.1) | collective-permute-done | bytes 2097184 | tf_op jit(solution)/shard_map/ppermute | solution.py:101
  715.5 44.9 %collective-permute-done.2 = f32[4096,128]{1,0:T(8,128)S(1)} collective-permute-done((f32[4096,128]{1,0:T(8,128)S(1)}, f32[4096,128]{1,0:T(8,128)S(1)}, u32[]{:S(2)}, u32[]{:S(2)}) %collective-permute-start.2) | collective-permute-done | bytes 2097184 | tf_op jit(solution)/shard_map/ppermute | solution.py:101
  768.1 10.5 %fusion.10 = f32[64,16384]{1,0:T(8,128)} fusion(bf16[32,8,128,128]{3,2,1,0:T(8,128)(2,1)} %bitcast.12, s32[256]{0:T(256)S(1)} %copy-done.10), kind=kOutput, calls=%fused_computation.18 | convolution fusion | flops 536887296 | bytes 12583936 | tf_op jit(solution)/shard_map/dot_general | solution.py:94
  783.4 28.8 %collective-permute-done.3 = f32[4096,128]{1,0:T(8,128)} collective-permute-done((f32[4096,128]{1,0:T(8,128)}, f32[4096,128]{1,0:T(8,128)}, u32[]{:S(2)}, u32[]{:S(2)}) %collective-permute-start.3) | collective-permute-done | bytes 2097184 | tf_op jit(solution)/shard_map/ppermute | solution.py:101
  (153 shorter events, 129.9 us)
Async XLA Ops:
  7.2 25.1 %copy-start = (bf16[8192,128]{1,0:T(8,128)(2,1)S(1)}, bf16[8192,128]{1,0:T(8,128)(2,1)}, u32[]{:S(2)}) copy-start(bf16[8192,128]{1,0:T(8,128)(2,1)} %param.11) | copy-start | bytes 6291460
  32.0 8.6 %copy-start.9 = (s32[256]{0:T(256)}, s32[256]{0:T(256)S(1)}, u32[]{:S(2)}) copy-start(s32[256]{0:T(256)S(1)} %all_to_all.16) | copy-start | bytes 3076
  48.0 9.5 %copy-start.8 = (f32[4096]{0:T(1024)S(1)}, f32[4096]{0:T(1024)}, u32[]{:S(2)}) copy-start(f32[4096]{0:T(1024)} %param.12) | copy-start | bytes 49156
  48.0 104.9 %all-to-all-start.1 = ((bf16[256,128,128]{2,1,0:T(8,128)(2,1)}), bf16[256,128,128]{2,1,0:T(8,128)(2,1)}, u32[]{:S(2)}, u32[]{:S(2)}) async-start(bf16[256,128,128]{2,1,0:T(8,128)(2,1)} %broadcast_select_fusion), calls=%async_computation.1 | async-start | bytes 16777216 | tf_op jit(solution)/shard_map/all_to_all | solution.py:38
  54.1 116.5 %all-gather.2.cloned.1.call-start = ((), (), s32[]{:S(2)}) async-start(), calls=%async_computation.3 | async-start | bytes 1114112 | tf_op jit(solution)/shard_map/all_gather | solution.py:31
  173.0 8.0 copy-start.4
  212.4 8.0 copy-start.4
  239.9 9.2 %copy-start.2 = (bf16[512,8192]{1,0:T(8,128)(2,1)S(1)}, bf16[512,8192]{1,0:T(8,128)(2,1)}, u32[]{:S(2)}) copy-start(bf16[512,8192]{1,0:T(8,128)(2,1)} %fusion.39) | copy-start | bytes 25165828 | tf_op jit(solution)/shard_map/while
  239.9 9.2 %copy-start.5 = (bf16[8192,128]{1,0:T(8,128)(2,1)S(1)}, bf16[8192,128]{1,0:T(8,128)(2,1)}, u32[]{:S(2)}) copy-start(bf16[8192,128]{1,0:T(8,128)(2,1)} %get-tuple-element.328) | copy-start | bytes 6291460 | tf_op jit(solution)/shard_map/while
  253.1 8.0 copy-start.4
  280.6 9.2 %copy-start.2 = (bf16[512,8192]{1,0:T(8,128)(2,1)S(1)}, bf16[512,8192]{1,0:T(8,128)(2,1)}, u32[]{:S(2)}) copy-start(bf16[512,8192]{1,0:T(8,128)(2,1)} %fusion.39) | copy-start | bytes 25165828 | tf_op jit(solution)/shard_map/while
  280.6 9.2 %copy-start.5 = (bf16[8192,128]{1,0:T(8,128)(2,1)S(1)}, bf16[8192,128]{1,0:T(8,128)(2,1)}, u32[]{:S(2)}) copy-start(bf16[8192,128]{1,0:T(8,128)(2,1)} %get-tuple-element.328) | copy-start | bytes 6291460 | tf_op jit(solution)/shard_map/while
  293.8 8.0 copy-start.4
  321.3 9.2 %copy-start.2 = (bf16[512,8192]{1,0:T(8,128)(2,1)S(1)}, bf16[512,8192]{1,0:T(8,128)(2,1)}, u32[]{:S(2)}) copy-start(bf16[512,8192]{1,0:T(8,128)(2,1)} %fusion.39) | copy-start | bytes 25165828 | tf_op jit(solution)/shard_map/while
  321.3 9.2 %copy-start.5 = (bf16[8192,128]{1,0:T(8,128)(2,1)S(1)}, bf16[8192,128]{1,0:T(8,128)(2,1)}, u32[]{:S(2)}) copy-start(bf16[8192,128]{1,0:T(8,128)(2,1)} %get-tuple-element.328) | copy-start | bytes 6291460 | tf_op jit(solution)/shard_map/while
  361.9 9.2 %copy-start.2 = (bf16[512,8192]{1,0:T(8,128)(2,1)S(1)}, bf16[512,8192]{1,0:T(8,128)(2,1)}, u32[]{:S(2)}) copy-start(bf16[512,8192]{1,0:T(8,128)(2,1)} %fusion.39) | copy-start | bytes 25165828 | tf_op jit(solution)/shard_map/while
  361.9 9.2 %copy-start.5 = (bf16[8192,128]{1,0:T(8,128)(2,1)S(1)}, bf16[8192,128]{1,0:T(8,128)(2,1)}, u32[]{:S(2)}) copy-start(bf16[8192,128]{1,0:T(8,128)(2,1)} %get-tuple-element.328) | copy-start | bytes 6291460 | tf_op jit(solution)/shard_map/while
  375.1 8.0 copy-start.4
  402.6 9.2 %copy-start.2 = (bf16[512,8192]{1,0:T(8,128)(2,1)S(1)}, bf16[512,8192]{1,0:T(8,128)(2,1)}, u32[]{:S(2)}) copy-start(bf16[512,8192]{1,0:T(8,128)(2,1)} %fusion.39) | copy-start | bytes 25165828 | tf_op jit(solution)/shard_map/while
  402.6 9.2 %copy-start.5 = (bf16[8192,128]{1,0:T(8,128)(2,1)S(1)}, bf16[8192,128]{1,0:T(8,128)(2,1)}, u32[]{:S(2)}) copy-start(bf16[8192,128]{1,0:T(8,128)(2,1)} %get-tuple-element.328) | copy-start | bytes 6291460 | tf_op jit(solution)/shard_map/while
  443.3 9.2 %copy-start.2 = (bf16[512,8192]{1,0:T(8,128)(2,1)S(1)}, bf16[512,8192]{1,0:T(8,128)(2,1)}, u32[]{:S(2)}) copy-start(bf16[512,8192]{1,0:T(8,128)(2,1)} %fusion.39) | copy-start | bytes 25165828 | tf_op jit(solution)/shard_map/while
  443.3 9.2 %copy-start.5 = (bf16[8192,128]{1,0:T(8,128)(2,1)S(1)}, bf16[8192,128]{1,0:T(8,128)(2,1)}, u32[]{:S(2)}) copy-start(bf16[8192,128]{1,0:T(8,128)(2,1)} %get-tuple-element.328) | copy-start | bytes 6291460 | tf_op jit(solution)/shard_map/while
  483.9 9.2 %copy-start.2 = (bf16[512,8192]{1,0:T(8,128)(2,1)S(1)}, bf16[512,8192]{1,0:T(8,128)(2,1)}, u32[]{:S(2)}) copy-start(bf16[512,8192]{1,0:T(8,128)(2,1)} %fusion.39) | copy-start | bytes 25165828 | tf_op jit(solution)/shard_map/while
  483.9 9.2 %copy-start.5 = (bf16[8192,128]{1,0:T(8,128)(2,1)S(1)}, bf16[8192,128]{1,0:T(8,128)(2,1)}, u32[]{:S(2)}) copy-start(bf16[8192,128]{1,0:T(8,128)(2,1)} %get-tuple-element.328) | copy-start | bytes 6291460 | tf_op jit(solution)/shard_map/while
  512.6 11.4 %copy-start.3 = (f32[4096,128]{1,0:T(8,128)S(1)}, f32[4096,128]{1,0:T(8,128)}, u32[]{:S(2)}) copy-start(f32[4096,128]{1,0:T(8,128)} %get-tuple-element.172) | copy-start | bytes 6291460
  512.6 255.4 %all-to-all-start.2 = ((bf16[256,128,128]{2,1,0:T(8,128)(2,1)}), bf16[256,128,128]{2,1,0:T(8,128)(2,1)}, u32[]{:S(2)}, u32[]{:S(2)}) async-start(bf16[256,128,128]{2,1,0:T(8,128)(2,1)} %scatter_fusion), calls=%async_computation.2 | async-start | bytes 16777216 | tf_op jit(solution)/shard_map/all_to_all | solution.py:90
  524.0 138.7 %collective-permute-start = (f32[4096,128]{1,0:T(8,128)S(1)}, f32[4096,128]{1,0:T(8,128)S(1)}, u32[]{:S(2)}, u32[]{:S(2)}) collective-permute-start(f32[4096,128]{1,0:T(8,128)S(1)} %copy-done.3), channel_id=1, source_target_pairs={{0,1},{1,0},{2,3},{3,2},{4,5},{5,4},{6,7},{7,6},{8,9},{9,8},{10,11... | collective-permute-start | bytes 6291464 | tf_op jit(solution)/shard_map/ppermute | solution.py:101
  664.6 49.0 %collective-permute-start.1 = (f32[4096,128]{1,0:T(8,128)S(1)}, f32[4096,128]{1,0:T(8,128)S(1)}, u32[]{:S(2)}, u32[]{:S(2)}) collective-permute-start(f32[4096,128]{1,0:T(8,128)S(1)} %add.107), channel_id=1, source_target_pairs={{0,2},{1,3},{2,0},{3,1},{4,6},{5,7},{6,4},{7,5},{8,10},{9,11},{10,... | collective-permute-start | bytes 6291464 | tf_op jit(solution)/shard_map/ppermute | solution.py:101
  713.8 54.2 %copy-start.10 = (s32[256]{0:T(256)S(1)}, s32[256]{0:T(256)}, u32[]{:S(2)}) copy-start(s32[256]{0:T(256)} %copy-done.9) | copy-start | bytes 3076
  713.8 46.6 %collective-permute-start.2 = (f32[4096,128]{1,0:T(8,128)S(1)}, f32[4096,128]{1,0:T(8,128)S(1)}, u32[]{:S(2)}, u32[]{:S(2)}) collective-permute-start(f32[4096,128]{1,0:T(8,128)S(1)} %add.108), channel_id=1, source_target_pairs={{0,4},{1,5},{2,6},{3,7},{4,0},{5,1},{6,2},{7,3},{8,12},{9,13},{10,... | collective-permute-start | bytes 6291464 | tf_op jit(solution)/shard_map/ppermute | solution.py:101
  762.0 50.2 %collective-permute-start.3 = (f32[4096,128]{1,0:T(8,128)}, f32[4096,128]{1,0:T(8,128)}, u32[]{:S(2)}, u32[]{:S(2)}) collective-permute-start(f32[4096,128]{1,0:T(8,128)} %add.109), channel_id=1, source_target_pairs={{0,8},{1,9},{2,10},{3,11},{4,12},{5,13},{6,14},{7,15},{8,0},{9,1},... | collective-permute-start | bytes 6291464 | tf_op jit(solution)/shard_map/ppermute | solution.py:101
  768.1 45.9 %copy-start.1 = (bf16[8192,128]{1,0:T(8,128)(2,1)S(1)}, bf16[8192,128]{1,0:T(8,128)(2,1)}, u32[]{:S(2)}) copy-start(bf16[8192,128]{1,0:T(8,128)(2,1)} %param.11) | copy-start | bytes 6291460
  (7 other events, 54.2 us)
Sparse Core Ops, SparseCore 0:
  57.1 113.4 all-gather.1
